TPU v7x, 32 devices: a whole 2x2x4 slice. The times are simulated.
32 devices in a mesh: row: 4 (over z), col: 8 (over y, x, core).
Axes of the slice: x: 2, y: 2, z: 4, core: 2. Of those that a mesh axis runs over, the one named last changes fastest.
Arguments:
- precision_diag: float32 [32, 256, 256], P(('row', 'col')), may hold values from -0.1 to 4.6, as said below
- precision_pairs: float32 [32, 7, 256, 256], P(('row', 'col')), may hold values from -0.024 to 0.024
- pattern_cols: int32 [32, 7], P(('row', 'col')), may hold values from -1 to 31, as said below
- newton_diag: float32 [32, 256, 256], P(('row', 'col')), may hold values from -0.1 to 0.1, as said below
- newton_pairs: float32 [32, 7, 256, 256], P(('row', 'col')), may hold values from -0.006 to 0.006
- warm_start: float32 [32, 96, 256], P(('row', 'col')), may hold values from -15 to 15
- target_rows: int32 [96], replicated, may hold values from 0 to 8191, as said below
Outputs:
- inverse_panel: float32 [32, 96, 256], P(('row', 'col'))
- hessian_block: float32 [96, 96], P('row', 'col')
Inputs may be any that keep to these rules, and one draw needn't show every extreme that they name: `pattern_cols`: each row lists its live entries first and -1 for the rest; it has 4 to 7 live entries, some row exactly 7 and some fewer. The live entries of block row I are distinct, differ from I, and lie in the group of 8 consecutive block rows that holds I (groups start at multiples of 8). `precision_diag`: each tile is symmetric, and X is positive definite. `newton_diag`: each tile is symmetric. `target_rows`: the 96 entries are distinct rows of X.
All inputs are finite; a program needn't handle non-finite values.
Results may differ from a plain program's by a relative error of at most 0.0003.
Values sent between devices are 32-bit elements; how exact they have to be, the bound alone decides.
No kernel may reach another device: no remote copies, remote signals or barrier semaphores. Data moves between devices by JAX's collectives and lax.ppermute only.
A program may use at most 64 MiB of HBM per device.

v0:
```python
import jax
import jax.numpy as jnp
from jax import lax
from jax.sharding import PartitionSpec as P

HIGHEST = lax.Precision.HIGHEST


def route_buffer(pair_tiles, local_cols, live_mask, cols_count):
    rows_dev = pair_tiles.shape[0]
    block_size = pair_tiles.shape[2]
    targets = jnp.arange(cols_count * rows_dev, dtype=jnp.int32)
    matches = ((local_cols[:, :, None] == targets[None, None, :]) & live_mask[:, :, None]).astype(
        jnp.float32
    )
    outgoing = jnp.einsum("rkg,rkab->grab", matches, pair_tiles, precision=HIGHEST)
    return outgoing.reshape((cols_count * rows_dev * rows_dev, block_size, block_size))


def apply_blocks(blocks, diag_tiles, pair_tiles, local_cols, weights, routed):
    gathered = lax.all_gather(blocks, "col", axis=0, tiled=True)
    picked = jnp.take(gathered, local_cols, axis=0) * weights
    own_rows = jnp.einsum("icb,iab->ica", blocks, diag_tiles, precision=HIGHEST)
    own_rows = own_rows + jnp.einsum("ikcb,ikab->ica", picked, pair_tiles, precision=HIGHEST)
    rows_dev = blocks.shape[0]
    sources = gathered.shape[0] // rows_dev
    block_size = blocks.shape[2]
    panels = gathered.reshape((sources, rows_dev) + blocks.shape[1:])
    tiles = routed.reshape((sources, rows_dev, rows_dev, block_size, block_size))
    incoming = jnp.einsum("srcb,sqrba->qca", panels, tiles, precision=HIGHEST)
    return own_rows + incoming


def column_dots(first, second):
    return jnp.sum(first * second, axis=(0, 2))


def residual_norm(residual):
    return lax.psum(column_dots(residual, residual), ("row", "col"))


def on_device(
    precision_diag,
    precision_pairs,
    pattern_cols,
    newton_diag,
    newton_pairs,
    warm_start,
    target_rows,
):
    rows_dev = warm_start.shape[0]
    block_size = warm_start.shape[2]
    cols_count = lax.axis_size("col")
    first_block = (lax.axis_index("row") * cols_count + lax.axis_index("col")) * rows_dev
    group_first = lax.axis_index("row") * cols_count * rows_dev
    live_mask = pattern_cols >= 0
    local_cols = jnp.where(live_mask, pattern_cols - group_first, 0)
    weights = live_mask.astype(jnp.float32)[:, :, None, None]
    global_rows = (
        first_block * block_size + jnp.arange(rows_dev * block_size, dtype=jnp.int32)
    ).reshape(rows_dev, 1, block_size)
    unit_columns = (global_rows == target_rows[None, :, None]).astype(jnp.float32)
    precision_routed = lax.all_to_all(
        route_buffer(precision_pairs, local_cols, live_mask, cols_count),
        "col",
        split_axis=0,
        concat_axis=0,
        tiled=True,
    )

    def precision_apply(blocks):
        return apply_blocks(
            blocks, precision_diag, precision_pairs, local_cols, weights, precision_routed
        )

    solution = warm_start
    residual = unit_columns - precision_apply(solution)
    norm_now = residual_norm(residual)
    direction = residual
    for iteration in range(2):
        images = precision_apply(direction)
        curvature = lax.psum(column_dots(direction, images), ("row", "col"))
        step_size = norm_now / curvature
        solution = solution + step_size[None, :, None] * direction
        if iteration == 0:
            residual = residual - step_size[None, :, None] * images
            norm_next = residual_norm(residual)
            direction = residual + (norm_next / norm_now)[None, :, None] * direction
            norm_now = norm_next
    newton_delivered = lax.all_to_all(
        route_buffer(newton_pairs, local_cols, live_mask, cols_count),
        "col",
        split_axis=0,
        concat_axis=0,
        tiled=True,
    )
    newton_image = apply_blocks(
        solution, newton_diag, newton_pairs, local_cols, weights, newton_delivered
    )
    hessian_fragment = jnp.einsum("icb,idb->cd", solution, newton_image, precision=HIGHEST)
    spread_cols = lax.psum_scatter(hessian_fragment, "col", scatter_dimension=1, tiled=True)
    hessian = lax.psum_scatter(spread_cols, "row", scatter_dimension=0, tiled=True)
    return (solution, hessian)


def solution(mesh):
    placed = (
        P(("row", "col"), None, None),
        P(("row", "col"), None, None, None),
        P(("row", "col"), None),
        P(("row", "col"), None, None),
        P(("row", "col"), None, None, None),
        P(("row", "col"), None, None),
        P(),
    )
    return jax.shard_map(
        on_device,
        mesh=mesh,
        in_specs=placed,
        out_specs=(P(("row", "col"), None, None), P("row", "col")),
        check_vma=False,
    )
```

profile of v0, /device:TPU:0, one launch (start us, length us, event | category | flops | bytes accessed | tf_op | source)
XLA Modules:
  0.0 275.3 jit_solution(4029857724638175436)
XLA Ops:
  2.2 2.4 fusion.3
  4.6 2.0 copy.16
  6.6 5.2 %all-to-all-start = ((f32[8,256,256]{2,1,0:T(8,128)}), f32[8,256,256]{2,1,0:T(8,128)}, u32[]{:S(2)}, u32[]{:S(2)}) async-start(f32[8,256,256]{2,1,0:T(8,128)} %copy.16), calls=%async_computation | async-start | bytes 4194304 | tf_op jit(solution)/shard_map/all_to_all | solution.py:63
  11.8 3.9 %fusion.1 = f32[8,256,256]{2,0,1:T(8,128)S(1)} fusion(f32[7,256,256]{2,1,0:T(8,128)} %bitcast.166, s32[7]{0:T(128)S(1)} %bitcast.168, pred[7]{0:T(512)(128)(4,1)S(1)} %get-tuple-element.9), kind=kOutput, calls=%fused_computation.4 | convolution fusion | flops 44040304 | bytes 3932195 | tf_op jit(solution)/shard_map/rkg,rkab->grab/dot_general | solution.py:16
  15.7 1.9 copy.19
  17.6 26.2 %all_gather.12 = f32[8,96,256]{2,1,0:T(8,128)S(1)} all-gather(f32[1,96,256]{2,1,0:T(8,128)S(1)} %copy-done.5), channel_id=1, replica_groups=mesh['row'=4,'col'=8] {'col'}, dimensions={0}, use_global_device_ids=true | all-gather | bytes 884736 | tf_op jit(solution)/shard_map/all_gather | solution.py:21
  44.5 1.8 convolution_bitcast_fusion.7
  46.7 4.3 %all-to-all-start.1 = ((f32[8,256,256]{2,1,0:T(8,128)}), f32[8,256,256]{2,1,0:T(8,128)}, u32[]{:S(2)}, u32[]{:S(2)}) async-start(f32[8,256,256]{2,1,0:T(8,128)} %copy.19), calls=%async_computation.1 | async-start | bytes 4194304 | tf_op jit(solution)/shard_map/all_to_all | solution.py:90
  51.1 2.9 %fusion.11 = f32[1,96,256]{2,1,0:T(8,128)S(1)} fusion(f32[1,96,256]{2,1,0:T(8,128)S(1)} %fusion.15, f32[8,256,256]{2,1,0:T(8,128)} %all-to-all-done, f32[8,96,256]{2,1,0:T(8,128)S(1)} %all_gather.12, s32[256]{0:T(256)S(1)} %iota_add_fusion, s32[96]{0:T(128)S(1)} %copy-done.8), kind=kOutput, calls=%fused_computation.18 | convolution fusion | flops 604078080 | bytes 3081600 | tf_op jit(solution)/shard_map/srcb,sqrba->qca/dot_general | solution.py:30
  53.9 29.1 %all_gather.13 = f32[8,96,256]{2,1,0:T(8,128)S(1)} all-gather(f32[1,96,256]{2,1,0:T(8,128)S(1)} %fusion.11), channel_id=1, replica_groups=mesh['row'=4,'col'=8] {'col'}, dimensions={0}, use_global_device_ids=true | all-gather | bytes 884736 | tf_op jit(solution)/shard_map/all_gather | solution.py:21
  83.6 1.8 convolution_bitcast_fusion.6
  85.9 3.0 %multiply_reduce_fusion.1 = (f32[96]{0:T(128)S(1)}, f32[96]{0:T(128)S(1)}, f32[1,96,256]{2,1,0:T(8,128)S(1)}) fusion(f32[1,96,256]{2,1,0:T(8,128)S(1)} %fusion.11, f32[1,96,256]{2,1,0:T(8,128)S(1)} %fusion.14, f32[8,256,256]{2,1,0:T(8,128)} %all-to-all-done, f32[8,96,256]{2,1,0:T(8,128)S(1)} %all_gather.13), kind=kOutput, calls=%fused_computation.70 | convolution fusion | flops 604102464 | bytes 3179264 | tf_op jit(solution)/shard_map/srcb,sqrba->qca/dot_general | solution.py:30
  88.8 40.1 %all-reduce.3 = (f32[96]{0:T(128)S(1)}, f32[96]{0:T(128)S(1)}) all-reduce(f32[96]{0:T(128)S(1)} %get-tuple-element.4, f32[96]{0:T(128)S(1)} %get-tuple-element.3), channel_id=1, replica_groups=mesh['row'=4,'col'=8] {'row','col'}, use_global_device_ids=true, to_apply=%region_1.3 | all-reduce | flops 192 | bytes 1536 | tf_op jit(solution)/shard_map/psum | solution.py:39
  129.1 39.8 %psum.30 = f32[96]{0:T(128)S(1)} all-reduce(f32[96]{0:T(128)S(1)} %multiply_reduce_fusion), channel_id=1, replica_groups=mesh['row'=4,'col'=8] {'row','col'}, use_global_device_ids=true, to_apply=%region_5.7 | all-reduce | flops 96 | bytes 768 | tf_op jit(solution)/shard_map/psum | solution.py:39
  169.0 11.2 %all_gather.14 = f32[8,96,256]{2,1,0:T(8,128)S(1)} all-gather(f32[1,96,256]{2,1,0:T(8,128)S(1)} %multiply_add_fusion.1), channel_id=1, replica_groups=mesh['row'=4,'col'=8] {'col'}, dimensions={0}, use_global_device_ids=true | all-gather | bytes 884736 | tf_op jit(solution)/shard_map/all_gather | solution.py:21
  180.8 1.8 convolution_bitcast_fusion.5
  183.0 3.0 %fusion.16 = f32[96]{0:T(128)S(1)} fusion(f32[1,96,256]{2,1,0:T(8,128)S(1)} %multiply_add_fusion.1, f32[1,96,256]{2,1,0:T(8,128)S(1)} %fusion.13, f32[8,256,256]{2,1,0:T(8,128)} %all-to-all-done, f32[8,96,256]{2,1,0:T(8,128)S(1)} %all_gather.14), kind=kOutput, calls=%fused_computation.31 | convolution fusion | flops 604053376 | bytes 3080576 | tf_op jit(solution)/shard_map/srcb,sqrba->qca/dot_general | solution.py:30
  186.0 38.3 %psum.31 = f32[96]{0:T(128)S(1)} all-reduce(f32[96]{0:T(128)S(1)} %fusion.16), channel_id=1, replica_groups=mesh['row'=4,'col'=8] {'row','col'}, use_global_device_ids=true, to_apply=%region_7.9 | all-reduce | flops 96 | bytes 768 | tf_op jit(solution)/shard_map/psum | solution.py:82
  224.4 11.4 %all_gather.15 = f32[8,96,256]{2,1,0:T(8,128)S(1)} all-gather(f32[1,96,256]{2,1,0:T(8,128)S(1)} %multiply_add_fusion), channel_id=1, replica_groups=mesh['row'=4,'col'=8] {'col'}, dimensions={0}, use_global_device_ids=true | all-gather | bytes 884736 | tf_op jit(solution)/shard_map/all_gather | solution.py:21
  236.4 3.4 %convolution_bitcast_fusion.4 = f32[96,256]{1,0:T(8,128)S(1)} fusion(f32[7,96,256]{2,1,0:T(8,128)S(1)} %gather_fusion.3, f32[7]{0:T(128)S(1)} %get-tuple-element.10, pred[7]{0:T(512)(128)(4,1)S(1)} %get-tuple-element.11, f32[1,7,256,256]{3,2,1,0:T(8,128)} %param.13), kind=kOutput, calls=%fused_computation.19 | convolution fusion | flops 528826368 | bytes 2621475 | tf_op jit(solution)/shard_map/ikcb,ikab->ica/dot_general | solution.py:24
  240.2 2.9 %fusion.6 = f32[96,256]{1,0:T(8,128)S(1)} fusion(f32[1,96,256]{2,1,0:T(8,128)S(1)} %fusion.12, f32[8,256,256]{2,1,0:T(8,128)} %all-to-all-done.1, f32[8,96,256]{2,1,0:T(8,128)S(1)} %all_gather.15), kind=kOutput, calls=%fused_computation.10 | convolution fusion | flops 604004352 | bytes 3080192 | tf_op jit(solution)/shard_map/srcb,sqrba->qca/dot_general | solution.py:30
  243.3 14.7 %fusion = f32[96,16]{0,1:T(8,128)S(1)} fusion(f32[96,96]{0,1:T(8,128)S(1)} %fusion.45), kind=kCustom, calls=%all-reduce-scatter | all-reduce-scatter fusion | flops 12289 | bytes 43520
  259.3 1.9 collective-permute-start.1
  264.0 10.6 %all-reduce.1 = f32[96,12]{0,1:T(8,128)S(1)} all-reduce(f32[96,12]{0,1:T(8,128)S(1)} %constant_dynamic-slice_fusion), channel_id=3, replica_groups=mesh['row'=4,'col'=8] {'row'}, use_global_device_ids=true, to_apply=%region_9.11.clone | all-reduce | flops 1152 | bytes 9216
  (52 shorter events, 9.5 us)
Async XLA Ops:
  0.6 1.5 copy-start
  6.6 40.1 %all-to-all-start = ((f32[8,256,256]{2,1,0:T(8,128)}), f32[8,256,256]{2,1,0:T(8,128)}, u32[]{:S(2)}, u32[]{:S(2)}) async-start(f32[8,256,256]{2,1,0:T(8,128)} %copy.16), calls=%async_computation | async-start | bytes 4194304 | tf_op jit(solution)/shard_map/all_to_all | solution.py:63
  15.6 2.0 copy-start.5
  44.4 1.9 copy-start.1
  46.7 4.4 %copy-start.8 = (s32[96]{0:T(128)S(1)}, s32[96]{0:T(128)}, u32[]{:S(2)}) copy-start(s32[96]{0:T(128)} %param.15) | copy-start | bytes 1156
  46.7 193.5 %all-to-all-start.1 = ((f32[8,256,256]{2,1,0:T(8,128)}), f32[8,256,256]{2,1,0:T(8,128)}, u32[]{:S(2)}, u32[]{:S(2)}) async-start(f32[8,256,256]{2,1,0:T(8,128)} %copy.19), calls=%async_computation.1 | async-start | bytes 4194304 | tf_op jit(solution)/shard_map/all_to_all | solution.py:90
  83.6 1.8 copy-start.2
  180.8 1.8 copy-start.3
  182.6 41.6 %copy-start.6 = (f32[1,96,256]{2,1,0:T(8,128)S(1)}, f32[1,96,256]{2,1,0:T(8,128)}, u32[]{:S(2)}) copy-start(f32[1,96,256]{2,1,0:T(8,128)} %param.14) | copy-start | bytes 294916
  224.4 18.7 %copy-start.4 = (f32[1,96,256]{2,1,0:T(8,128)}, f32[1,96,256]{2,1,0:T(8,128)S(1)}, u32[]{:S(2)}) copy-start(f32[1,96,256]{2,1,0:T(8,128)S(1)} %multiply_add_fusion) | copy-start | bytes 294916
  236.4 3.4 %copy-start.7 = (f32[1,256,256]{2,1,0:T(8,128)S(1)}, f32[1,256,256]{2,1,0:T(8,128)}, u32[]{:S(2)}) copy-start(f32[1,256,256]{2,1,0:T(8,128)} %param.12) | copy-start | bytes 786436
  239.8 21.4 %copy-start.9 = (u32[32]{0:T(128)S(1)}, u32[32]{0:T(128)}, u32[]{:S(2)}) copy-start(u32[32]{0:T(128)} %constant.35) | copy-start | bytes 388
  239.8 22.7 %copy-start.10 = (u32[32]{0:T(128)S(1)}, u32[32]{0:T(128)}, u32[]{:S(2)}) copy-start(u32[32]{0:T(128)} %constant.39) | copy-start | bytes 388
  258.0 5.7 %collective-permute-start = (f32[96,16]{0,1:T(8,128)S(1)}, f32[96,16]{0,1:T(8,128)S(1)}, u32[]{:S(2)}, u32[]{:S(2)}) collective-permute-start(f32[96,16]{0,1:T(8,128)S(1)} %fusion), channel_id=1, source_target_pairs={{0,1},{1,2},{2,3},{3,4},{4,5},{5,6},{6,7},{8,9},{9,10},{10,11},{11... | collective-permute-start | bytes 18440
  259.3 4.4 %collective-permute-start.1 = (f32[96,12]{0,1:T(8,128)S(1)}, f32[96,12]{0,1:T(8,128)S(1)}, u32[]{:S(2)}, u32[]{:S(2)}) collective-permute-start(f32[96,12]{0,1:T(8,128)S(1)} %slice.8), channel_id=1, source_target_pairs={{0,2},{1,3},{2,4},{3,5},{4,6},{5,7},{8,10},{9,11},{10,12},{11,13},... | collective-permute-start | bytes 13832
where the time goes:
time: 277 us; the launch traced here: 275 us
  blocking collectives  221 us (80%)
  matrix products  28.6 us (10%)
  starting transfers between devices  12.7 us (5%)
  local copies, waits for them, and re-layouts  9.16 us (3%)
    psum x2, blocking collectives, residual_norm(): return lax.psum(column_dots(residual, residual), ('row', 'col'))  79.9 us
    all_gather x4, blocking collectives, apply_blocks(): gathered = lax.all_gather(blocks, 'col', axis=0, tiled=True)  77.9 us
    psum x1, blocking collectives, on_device(): curvature = lax.psum(column_dots(direction, images), ('row', 'col'))  38.3 us
    unnamed x2, blocking collectives  25.3 us
    dot_general x4, matrix products, apply_blocks(): incoming = jnp.einsum('srcb,sqrba->qca', panels, tiles, precision=HIGHEST)  11.7 us
    dot_general x4, matrix products, apply_blocks(): jnp.einsum('ikcb,ikab->ica', picked, pair_tiles, precision=HIGHEST)  8.81 us
    dot_general x2, matrix products, route_buffer(): jnp.einsum('rkg,rkab->grab', matches, pair_tiles, precision=HIGHEST)  6.31 us
  transfers between devices with their start and end apart: 4, of which 0 were waited for; matrix products, arithmetic and copies ran while one was open for 11% of the time, Pallas kernels for 0%

commit v1 on v0

v1 whole, which is shorter than its diff:
```python
import functools

import jax
import jax.numpy as jnp
from jax import lax
from jax.experimental import pallas as pl
from jax.experimental.pallas import tpu as pltpu
from jax.sharding import Mesh, PartitionSpec as P

F32 = jnp.float32
BF16 = jnp.bfloat16
ALL = ("row", "chip", "core")
VMEM_LIMIT = 24 << 20
LANES = 128
HALF = 64

NT = (((1,), (1,)), ((), ()))
NN = (((1,), (0,)), ((), ()))


def split(value):
    high = value.astype(BF16)
    low = (value - high.astype(F32)).astype(BF16)
    return high, low


def dot3(left, right, dims):
    rows = left[0].shape[0]
    both = jnp.concatenate(left, axis=0)
    first = lax.dot_general(both, right[0], dims, preferred_element_type=F32)
    second = lax.dot_general(left[0], right[1], dims, preferred_element_type=F32)
    return first[:rows] + first[rows:] + second


def row_sums(product):
    ones = jnp.ones((8, product.shape[1]), F32)
    sums = lax.dot_general(
        ones, product, NT, precision=lax.Precision.HIGHEST, preferred_element_type=F32
    )
    return sums[0:1]


def column_of(row):
    n = row.shape[1]
    eye = lax.broadcasted_iota(jnp.int32, (n, n), 0) == lax.broadcasted_iota(
        jnp.int32, (n, n), 1
    )
    return jnp.sum(jnp.where(eye, row, 0.0), axis=1, keepdims=True)


def contributions(slots, core, tiles, panel, keep, send):
    keep[...] = jnp.zeros_like(keep)
    send[...] = jnp.zeros_like(send)
    for k in range(tiles.shape[0]):
        slot = slots[k]

        @pl.when(slot >= 0)
        def _():
            value = dot3(panel, split(tiles[k]), NN)
            chip = slot // 2

            @pl.when(slot % 2 == core)
            def _():
                keep[chip] = value

            @pl.when(slot % 2 != core)
            def _():
                send[chip] = value


def half_apply(slots, core, tiles, diag, panel, same, other, acc):
    acc[...] = dot3(panel, split(diag[...]), NT) * 0.5
    for k in range(tiles.shape[0]):
        slot = slots[k]

        @pl.when(slot >= 0)
        def _():
            chip = slot // 2
            picked = jnp.where(slot % 2 == core, same[chip], other[chip])
            acc[...] += dot3(split(picked), split(tiles[k]), NT)


def first_kernel(meta, tiles, panel, keep, send):
    contributions(meta, meta[tiles.shape[0]], tiles, split(panel[...]), keep, send)


def pack_kernel(panel, keep, received, out):
    value = panel[...]
    for chip in range(keep.shape[0]):
        out[0, chip] = value
        out[1, chip] = keep[chip] + received[chip]


def residual_kernel(
    meta, tiles, diag, panel, both, other, target, residual, keep, send, acc
):
    core = meta[tiles.shape[0]]
    parts = split(panel[...])
    half_apply(meta, core, tiles, diag, parts, both.at[0], other, acc)
    total = acc[...] + dot3(parts, split(diag[...]), NT) * 0.5
    for chip in range(both.shape[1]):
        total = total + both[1, chip]
    rows, size = panel.shape
    unit = target[...] == lax.broadcasted_iota(jnp.int32, (rows, size), 1)
    value = unit.astype(F32) - total
    residual[...] = value
    contributions(meta, core, tiles, split(value), keep, send)


def image_kernel(
    meta, tiles, diag, panel, both, other, image, half, sums
):
    core = meta[tiles.shape[0]]
    value = panel[...]
    parts = split(value)
    half_apply(meta, core, tiles, diag, parts, both.at[0], other, half)
    total = half[...] + dot3(parts, split(diag[...]), NT) * 0.5
    for chip in range(both.shape[1]):
        total = total + both[1, chip]
    image[...] = total
    sums[0:1] = row_sums(value * value)
    sums[1:2] = row_sums(value * total)
    sums[2:3] = row_sums(total * total)


def half_kernel(meta, tiles, diag, panel, both, other, out):
    half_apply(
        meta, meta[tiles.shape[0]], tiles, diag, split(panel[...]), both.at[0], other, out
    )


def all_half(slots, tiles, diag, panel, gathered, acc):
    acc[...] = dot3(panel, split(diag[...]), NT) * 0.5
    for k in range(tiles.shape[0]):
        slot = slots[k]

        @pl.when(slot >= 0)
        def _():
            acc[...] += dot3(split(gathered[slot]), split(tiles[k]), NT)


def middle_kernel(
    groups,
    parts_rows,
    parts_cols,
    meta,
    tiles,
    diag,
    newton_tiles,
    newton_diag,
    start,
    residual,
    image,
    gathered,
    half_residual,
    newton_start,
    newton_residual,
    sums,
    x_out,
    d_out,
    norm_out,
    packed,
    half_image,
    newton_image,
    left_pad,
    right_pad,
    blocks,
):
    image_parts = split(image[...])
    all_half(meta, tiles, diag, image_parts, gathered, half_image)
    all_half(meta, newton_tiles, newton_diag, image_parts, gathered, newton_image)
    totals = sums[0]
    for device in range(1, sums.shape[0]):
        totals = totals + sums[device]
    rr, rq, qq = totals[0:1], totals[1:2], totals[2:3]
    step = rr / rq
    norm = rr - 2.0 * step * rq + step * step * qq
    norm_out[...] = norm
    step_col = column_of(step)
    grow = 1.0 + column_of(norm / rr)
    r, q = residual[...], image[...]
    x1 = start[...] + step_col * r
    d1 = grow * r - step_col * q
    x_out[...] = x1
    d_out[...] = d1
    half_d = grow * half_residual[...] - step_col * half_image[...]
    curvature = 2.0 * row_sums(d1 * half_d)
    ux = newton_start[...] + step_col * newton_residual[...]
    ud = grow * newton_residual[...] - step_col * newton_image[...]
    rows = C = x1.shape[0]
    hr, hc = C // parts_rows, C // parts_cols
    total = None
    for side, (v, u) in enumerate(((x1, ux), (d1, ud))):
        left_pad[...] = jnp.zeros_like(left_pad)
        right_pad[...] = jnp.zeros_like(right_pad)
        for r_index in range(parts_rows):
            for kind, (v2, u2) in enumerate(((x1, ux), (d1, ud))):
                at = r_index * LANES + side * HALF + kind * hr
                left_pad[at : at + hr] = v2[r_index * hr : (r_index + 1) * hr]
                right_pad[at : at + hr] = u2[r_index * hr : (r_index + 1) * hr]
        term = dot3(split(v), split(right_pad[...]), NT) + dot3(
            split(u), split(left_pad[...]), NT
        )
        total = term if total is None else total + term
    blocks[...] = total
    for r_index in range(parts_rows):
        for c_index in range(parts_cols):
            at = r_index * parts_cols + c_index
            packed[at, 0:hc] = blocks[
                c_index * hc : (c_index + 1) * hc,
                r_index * LANES : (r_index + 1) * LANES,
            ]
            packed[at, hc : hc + 1, 0:C] = curvature
            packed[at, hc : hc + 1, C:LANES] = jnp.zeros((1, LANES - C), F32)


def last_kernel(parts_rows, parts_cols, meta, x1, d1, norm, received, x_out, hessian):
    total = received[0]
    for device in range(1, received.shape[0]):
        total = total + received[device]
    C = x1.shape[0]
    hr, hc = C // parts_rows, C // parts_cols
    step = norm[...] / total[hc : hc + 1, 0:C]
    step_col = column_of(step)
    x_out[...] = x1[...] + step_col * d1[...]
    row_at, col_at = meta[0] * hr, meta[1] * hc
    wanted = lax.broadcasted_iota(jnp.int32, (C, hr), 0) == row_at + lax.broadcasted_iota(
        jnp.int32, (C, hr), 1
    )
    of_rows = jnp.sum(jnp.where(wanted, step_col, 0.0), axis=0, keepdims=True)
    wanted = lax.broadcasted_iota(jnp.int32, (hc, C), 1) == col_at + lax.broadcasted_iota(
        jnp.int32, (hc, C), 0
    )
    of_cols = jnp.sum(jnp.where(wanted, step, 0.0), axis=1, keepdims=True)
    xx = total[0:hc, 0:hr]
    dx = total[0:hc, hr : 2 * hr]
    xd = total[0:hc, HALF : HALF + hr]
    dd = total[0:hc, HALF + hr : HALF + 2 * hr]
    hessian[...] = xx + of_rows * dx + of_cols * (xd + of_rows * dd)


def call(body, outs, scalars, arrays, scratch=(), flops=0):
    smem = pl.BlockSpec(memory_space=pltpu.SMEM)
    vmem = pl.BlockSpec(memory_space=pltpu.VMEM)
    shapes = [jax.ShapeDtypeStruct(s, F32) for s in outs]
    moved = sum(a.size * 4 for a in arrays)
    return pl.pallas_call(
        body,
        out_shape=shapes,
        in_specs=[smem] * len(scalars) + [vmem] * len(arrays),
        out_specs=[vmem] * len(shapes),
        scratch_shapes=[pltpu.VMEM(s, F32) for s in scratch],
        cost_estimate=pl.CostEstimate(
            flops=flops, bytes_accessed=moved, transcendentals=0
        ),
        compiler_params=pltpu.CompilerParams(vmem_limit_bytes=VMEM_LIMIT),
    )(*scalars, *arrays)


def on_device(
    precision_diag,
    precision_pairs,
    pattern_cols,
    newton_diag,
    newton_pairs,
    warm_start,
    target_rows,
):
    groups = lax.axis_size("row")
    chips = lax.axis_size("chip")
    columns = chips * 2
    devices = groups * columns
    row, chip, core = (lax.axis_index(a) for a in ALL)
    column = chip * 2 + core
    block = row * columns + column
    C, B = warm_start.shape[1:]
    slots = jnp.where(pattern_cols >= 0, pattern_cols - row * columns, -1)[0]
    meta = jnp.concatenate([slots, core[None].astype(jnp.int32)])
    place = jnp.concatenate([row[None], column[None]]).astype(jnp.int32)
    target = (target_rows - block * B).astype(jnp.int32)[:, None]
    tiles, diag = precision_pairs[0], precision_diag[0]
    ntiles, ndiag = newton_pairs[0], newton_diag[0]
    panel = (C, B)
    blocks = (chips, C, B)
    swap = [(0, 1), (1, 0)]
    unit = 2 * C * B * B * 3

    def exchange(value, keep, send):
        received = lax.ppermute(send, "core", swap)
        (packed,) = call(pack_kernel, [(2,) + blocks], [], [value, keep, received])
        both = lax.all_to_all(packed, "chip", 1, 1, tiled=True)
        other = lax.ppermute(both[0], "core", swap)
        return both, other

    start = warm_start[0]
    keep, send = call(
        first_kernel, [blocks, blocks], [meta], [tiles, start], flops=7 * unit
    )
    both_start, other_start = exchange(start, keep, send)
    residual, keep, send = call(
        residual_kernel,
        [panel, blocks, blocks],
        [meta],
        [tiles, diag, start, both_start, other_start, target],
        scratch=[panel],
        flops=15 * unit,
    )
    both_residual, other_residual = exchange(residual, keep, send)
    image, half_residual, sums = call(
        image_kernel,
        [panel, panel, (3, C)],
        [meta],
        [tiles, diag, residual, both_residual, other_residual],
        flops=8 * unit,
    )
    (newton_start,) = call(
        half_kernel,
        [panel],
        [meta],
        [ntiles, ndiag, start, both_start, other_start],
        flops=8 * unit,
    )
    (newton_residual,) = call(
        half_kernel,
        [panel],
        [meta],
        [ntiles, ndiag, residual, both_residual, other_residual],
        flops=8 * unit,
    )
    all_sums = lax.all_to_all(
        jnp.broadcast_to(sums[None], (devices,) + sums.shape), ALL, 0, 0, tiled=True
    )
    gathered = lax.all_gather(image, ("chip", "core"), axis=0, tiled=False)
    hc = C // columns
    depth = -(-(hc + 1) // 8) * 8
    x1, d1, norm, packed = call(
        functools.partial(middle_kernel, chips, groups, columns),
        [panel, panel, (1, C), (devices, depth, LANES)],
        [meta],
        [
            tiles,
            diag,
            ntiles,
            ndiag,
            start,
            residual,
            image,
            gathered,
            half_residual,
            newton_start,
            newton_residual,
            all_sums,
        ],
        scratch=[
            panel,
            panel,
            (groups * LANES, B),
            (groups * LANES, B),
            (C, groups * LANES),
        ],
        flops=20 * unit,
    )
    received = lax.all_to_all(packed, ALL, 0, 0, tiled=True)
    solved, hessian = call(
        functools.partial(last_kernel, groups, columns),
        [panel, (hc, C // groups)],
        [place],
        [x1, d1, norm, received],
        flops=unit // 100,
    )
    return solved[None], hessian.T


def solution(mesh):
    rows, columns = mesh.devices.shape
    fine = Mesh(mesh.devices.reshape(rows, columns // 2, 2), ALL)
    placed = (
        P(ALL, None, None),
        P(ALL, None, None, None),
        P(ALL, None),
        P(ALL, None, None),
        P(ALL, None, None, None),
        P(ALL, None, None),
        P(),
    )
    return jax.shard_map(
        on_device,
        mesh=fine,
        in_specs=placed,
        out_specs=(P(ALL, None, None), P("row", ("chip", "core"))),
        check_vma=False,
    )
```

time: 277 us -> 108 us (0.39)
  blocking collectives: 221 us -> 42 us
  matrix products: 28.6 us -> 0 us
  Pallas kernels: 0 us -> 22.4 us
  waiting for transfers between devices: 0.01 us -> 14.4 us
  local copies, waits for them, and re-layouts: 9.16 us -> 18.5 us
  starting transfers between devices: 12.7 us -> 9.43 us
    psum x3 -> x0, blocking collectives: 118 us -> none  [the longest x2 79.9 us: residual_norm(): return lax.psum(column_dots(residual, residual), ('row', 'col'))]
    all_gather x4 -> x1, blocking collectives: 77.9 us -> 11.1 us  [on_device(): gathered = lax.all_gather(image, ('chip', 'core'), axis=0, tiled=False)]
    all_to_all x0 -> x2, blocking collectives: none -> 30.9 us  [exchange(): both = lax.all_to_all(packed, 'chip', 1, 1, tiled=True)]
    dot_general x15 -> x0, matrix products: 28.6 us -> none  [the longest x4 11.7 us: apply_blocks(): incoming = jnp.einsum('srcb,sqrba->qca', panels, tiles, precision=HIGHEST)]
    unnamed x2 -> x0, blocking collectives: 25.3 us -> none
    pallas_call x0 -> x9, Pallas kernels: none -> 22.4 us  [call(): pl.pallas_call(body, out_shape=shapes, in_specs=[smem] * len(scalars) + [...]
    unnamed x28 -> x54, local copies, waits for them, and re-layouts: 2.89 us -> 15.5 us
    all_to_all x2, waiting for transfers between devices: 0.01 us -> 10.5 us  [the longest x1 10.5 us: on_device(): received = lax.all_to_all(packed, ALL, 0, 0, tiled=True)]
  transfers between devices with their start and end apart: 4 -> 6, of which waited for: 0 -> 4; matrix products, arithmetic and copies ran while one was open for 11% -> 1% of each run, Pallas kernels for 0% -> 5%
where the time goes in v1:
time: 108 us
  blocking collectives  42 us (39%)
  Pallas kernels  22.4 us (21%)
  local copies, waits for them, and re-layouts  18.5 us (17%)
  waiting for transfers between devices  14.4 us (13%)
  starting transfers between devices  9.43 us (9%)
    all_to_all x2, blocking collectives, exchange(): both = lax.all_to_all(packed, 'chip', 1, 1, tiled=True)  30.9 us
    pallas_call x9, Pallas kernels, call(): pl.pallas_call(body, out_shape=shapes, in_specs=[smem] * len(scalars) + [...  22.4 us
    unnamed x54, local copies, waits for them, and re-layouts  15.5 us
    all_gather x1, blocking collectives, on_device(): gathered = lax.all_gather(image, ('chip', 'core'), axis=0, tiled=False)  11.1 us
    all_to_all x1, waiting for transfers between devices, on_device(): received = lax.all_to_all(packed, ALL, 0, 0, tiled=True)  10.5 us
    all_to_all x1, starting transfers between devices, on_device(): lax.all_to_all(jnp.broadcast_to(sums[None], (devices,) + sums.shape), ALL...  4.74 us
    all_to_all x1, starting transfers between devices, on_device(): received = lax.all_to_all(packed, ALL, 0, 0, tiled=True)  4.48 us
    ppermute x2, waiting for transfers between devices, exchange(): received = lax.ppermute(send, 'core', swap)  3.42 us
  transfers between devices with their start and end apart: 6, of which 4 were waited for; matrix products, arithmetic and copies ran while one was open for 1% of the time, Pallas kernels for 5%

profile of v1, /device:TPU:0, one launch (start us, length us, event | category | flops | bytes accessed | tf_op | source)
XLA Modules:
  0.0 108.3 jit_solution(9115363700894905751)
XLA Ops:
  1.4 1.5 %copy-done = f32[1,7,256,256]{3,2,1,0:T(8,128)S(1)} copy-done((f32[1,7,256,256]{3,2,1,0:T(8,128)S(1)}, f32[1,7,256,256]{3,2,1,0:T(8,128)}, u32[]{:S(2)}) %copy-start) | copy-done | bytes 1835032
  3.8 2.1 %shard_map.86 = (f32[4,96,256]{2,1,0:T(8,128)S(1)}, f32[4,96,256]{2,1,0:T(8,128)S(1)}) custom-call(s32[8]{0:T(128)S(1)} %pad_add_fusion.1.meta, f32[7,256,256]{2,1,0:T(8,128)S(1)} %bitcast.19, f32[96,256]{1,0:T(8,128)S(1)} %bitcast.27), custom_call_target="tpu_custom_call" | custom-call | flops 264241152 | bytes 1933312 | tf_op jit(solution)/shard_map/pallas_call | solution.py:247
  5.9 1.7 %collective-permute-done.received = f32[4,96,256]{2,1,0:T(8,128)S(1)} collective-permute-done((f32[4,96,256]{2,1,0:T(8,128)S(1)}, f32[4,96,256]{2,1,0:T(8,128)S(1)}, u32[]{:S(2)}, u32[]{:S(2)}) %collective-permute-start) | collective-permute-done | bytes 393248 | tf_op jit(solution)/shard_map/ppermute | solution.py:289
  7.8 16.5 %all_to_all.20 = f32[2,4,96,256]{3,2,0,1:T(8,128)S(1)} all-to-all(f32[2,4,96,256]{3,2,0,1:T(8,128)S(1)} %copy.10), channel_id=1, replica_groups=mesh['row'=4,'chip'=4,'core'=2] {'chip'}, dimensions={1} | all-to-all | bytes 1572864 | tf_op jit(solution)/shard_map/all_to_all | solution.py:291
  25.4 1.2 %copy.12.both = f32[2,4,96,256]{3,2,1,0:T(8,128)S(1)} copy(f32[2,4,96,256]{3,2,0,1:T(8,128)} %copy-done.25) | data formatting | bytes 1572864 | tf_op jit(solution)/shard_map/all_to_all | solution.py:291
  27.1 4.3 %shard_map.88 = (f32[96,256]{1,0:T(8,128)S(1)}, f32[4,96,256]{2,1,0:T(8,128)S(1)}, f32[4,96,256]{2,1,0:T(8,128)S(1)}) custom-call(s32[8]{0:T(128)S(1)} %pad_add_fusion.1.meta, f32[7,256,256]{2,1,0:T(8,128)S(1)} %bitcast.20, f32[256,256]{1,0:T(8,128)S(1)} %bitcast.35, f32[96,256]{1,0:T(8,128)S(1)} %bitcast.29, f32[2,4,96,256]{3,2,1,0:T(8,128)S(1)} %copy.12.both, ...), custom_call_target="tpu_custom_call" | custom-call | flops 566231040 | bytes 3375488 | tf_op jit(solution)/shard_map/pallas_call | solution.py:247
  31.4 1.7 %collective-permute-done.2.received = f32[4,96,256]{2,1,0:T(8,128)S(1)} collective-permute-done((f32[4,96,256]{2,1,0:T(8,128)S(1)}, f32[4,96,256]{2,1,0:T(8,128)S(1)}, u32[]{:S(2)}, u32[]{:S(2)}) %collective-permute-start.2) | collective-permute-done | bytes 393248 | tf_op jit(solution)/shard_map/ppermute | solution.py:289
  33.3 14.5 %all_to_all.21 = f32[2,4,96,256]{3,2,0,1:T(8,128)S(1)} all-to-all(f32[2,4,96,256]{3,2,0,1:T(8,128)S(1)} %copy.14), channel_id=1, replica_groups=mesh['row'=4,'chip'=4,'core'=2] {'chip'}, dimensions={1} | all-to-all | bytes 1572864 | tf_op jit(solution)/shard_map/all_to_all | solution.py:291
  47.9 2.5 %shard_map.91.newton_start = f32[96,256]{1,0:T(8,128)S(1)} custom-call(s32[8]{0:T(128)S(1)} %pad_add_fusion.1.meta, f32[7,256,256]{2,1,0:T(8,128)S(1)} %bitcast.23, f32[256,256]{1,0:T(8,128)S(1)} %bitcast.32, f32[96,256]{1,0:T(8,128)S(1)} %bitcast.30, f32[2,4,96,256]{3,2,1,0:T(8,128)S(1)} %copy.12.both, f32[4,96,256]{2,1,0:T(8,128)S(1)} %collective-permute-done.1.other), custom_call_target="tpu_custom_call" | custom-call | flops 301989888 | bytes 3375104 | tf_op jit(solution)/shard_map/pallas_call | solution.py:247
  50.5 3.1 %shard_map.90 = (f32[96,256]{1,0:T(8,128)S(1)}, f32[96,256]{1,0:T(8,128)S(1)}, f32[3,96]{1,0:T(4,128)S(1)}) custom-call(s32[8]{0:T(128)S(1)} %pad_add_fusion.1.meta, f32[7,256,256]{2,1,0:T(8,128)S(1)} %bitcast.21, f32[256,256]{1,0:T(8,128)S(1)} %bitcast.36, f32[96,256]{1,0:T(8,128)S(1)} %get-tuple-element.18.panel.residual, ...), custom_call_target="tpu_custom_call" | custom-call | flops 301989888 | bytes 3375104 | tf_op jit(solution)/shard_map/pallas_call | solution.py:247
  54.3 4.7 %all-to-all-start.2 = ((f32[32,3,96]{2,1,0:T(4,128)}), f32[32,3,96]{2,1,0:T(4,128)}, u32[]{:S(2)}, u32[]{:S(2)}) async-start(f32[32,3,96]{2,1,0:T(4,128)} %broadcast_in_dim.30), calls=%async_computation.2 | async-start | bytes 131072 | tf_op jit(solution)/shard_map/all_to_all | solution.py:330
  59.1 11.1 %all-gather = f32[768,256]{1,0:T(8,128)S(1)} all-gather(f32[96,256]{1,0:T(8,128)} %copy-done.21), channel_id=2, replica_groups=mesh['row'=4,'chip'=4,'core'=2] {'chip','core'}, dimensions={0}, use_global_device_ids=true | all-gather | bytes 884736 | tf_op jit(solution)/shard_map/all_gather | solution.py:333
  70.1 1.5 %copy-done.3 = f32[1,7,256,256]{3,2,1,0:T(8,128)S(1)} copy-done((f32[1,7,256,256]{3,2,1,0:T(8,128)S(1)}, f32[1,7,256,256]{3,2,1,0:T(8,128)}, u32[]{:S(2)}) %copy-start.3) | copy-done | bytes 1835032
  71.6 0.9 copy-done.8
  73.5 1.0 copy-done.16
  74.5 2.5 %shard_map.92.newton_residual = f32[96,256]{1,0:T(8,128)S(1)} custom-call(s32[8]{0:T(128)S(1)} %pad_add_fusion.1.meta, f32[7,256,256]{2,1,0:T(8,128)S(1)} %bitcast.24, f32[256,256]{1,0:T(8,128)S(1)} %bitcast.33, f32[96,256]{1,0:T(8,128)S(1)} %copy-done.13, f32[2,4,96,256]{3,2,1,0:T(8,128)S(1)} %copy.16.both, f32[4,96,256]{2,1,0:T(8,128)S(1)} %copy-done.16), custom_call_target="tpu_custom_call" | custom-call | flops 301989888 | bytes 3375104 | tf_op jit(solution)/shard_map/pallas_call | solution.py:247
  77.6 1.5 %copy-done.4 = f32[1,7,256,256]{3,2,1,0:T(8,128)S(1)} copy-done((f32[1,7,256,256]{3,2,1,0:T(8,128)S(1)}, f32[1,7,256,256]{3,2,1,0:T(8,128)}, u32[]{:S(2)}) %copy-start.4) | copy-done | bytes 1835032
  79.1 0.9 copy-done.9
  80.1 0.9 copy-done.11
  81.0 0.9 copy-done.14
  85.5 6.3 %shard_map.93 = (f32[96,256]{1,0:T(8,128)S(1)}, f32[96,256]{1,0:T(8,128)S(1)}, f32[1,96]{1,0:T(1,128)S(1)}, f32[32,16,128]{2,1,0:T(8,128)}) custom-call(s32[8]{0:T(128)S(1)} %pad_add_fusion.1.meta, f32[7,256,256]{2,1,0:T(8,128)S(1)} %bitcast.22, f32[256,256]{1,0:T(8,128)S(1)} %bitcast.37, f32[7,256,256]{2,1,0:T(8,128)S(1)} %bitcast.25, ...), custom_call_target="tpu_custom_call" | custom-call | flops 754974720 | bytes 5607424 | tf_op jit(solution)/shard_map/pallas_call | solution.py:247
  91.9 4.5 %all-to-all-start.3 = ((f32[32,16,128]{2,1,0:T(8,128)}), f32[32,16,128]{2,1,0:T(8,128)S(1)}, u32[]{:S(2)}, u32[]{:S(2)}) async-start(f32[32,16,128]{2,1,0:T(8,128)} %get-tuple-element.27), calls=%async_computation.3 | async-start | bytes 524288 | tf_op jit(solution)/shard_map/all_to_all | solution.py:363
  96.4 10.5 %all-to-all-done.3.received = f32[32,16,128]{2,1,0:T(8,128)S(1)} async-done(((f32[32,16,128]{2,1,0:T(8,128)}), f32[32,16,128]{2,1,0:T(8,128)S(1)}, u32[]{:S(2)}, u32[]{:S(2)}) %all-to-all-start.3) | async-done | bytes 262176 | tf_op jit(solution)/shard_map/all_to_all | solution.py:363
  106.9 1.4 %shard_map.94 = (f32[96,256]{1,0:T(8,128)}, f32[12,24]{1,0:T(8,128)}) custom-call(s32[2]{0:T(128)S(1)} %pad_add_fusion.meta, f32[96,256]{1,0:T(8,128)S(1)} %get-tuple-element.24.x1, f32[96,256]{1,0:T(8,128)S(1)} %get-tuple-element.25.d1, f32[1,96]{1,0:T(1,128)S(1)} %get-tuple-element.26.norm, f32[32,16,128]{2,1,0:T(8,128)S(1)} %all-to-all-done.3.received), custom_call_target="tpu_custom_call" | custom-call | flops 377487 | bytes 459136 | tf_op jit(solution)/shard_map/pallas_call | solution.py:247
  (66 shorter events, 9.7 us)
Async XLA Ops:
  1.4 1.5 %copy-start = (f32[1,7,256,256]{3,2,1,0:T(8,128)S(1)}, f32[1,7,256,256]{3,2,1,0:T(8,128)}, u32[]{:S(2)}) copy-start(f32[1,7,256,256]{3,2,1,0:T(8,128)} %param.8) | copy-start | bytes 5505028
  5.9 1.8 %collective-permute-start = (f32[4,96,256]{2,1,0:T(8,128)S(1)}, f32[4,96,256]{2,1,0:T(8,128)S(1)}, u32[]{:S(2)}, u32[]{:S(2)}) collective-permute-start(f32[4,96,256]{2,1,0:T(8,128)S(1)} %get-tuple-element.17), channel_id=1, source_target_pairs={{0,1},{1,0},{2,3},{3,2},{4,5},{5,4},{6,7},{7,6},{8,9},{9,8},{10,11... | collective-permute-start | bytes 1179656 | tf_op jit(solution)/shard_map/ppermute | solution.py:289
  7.7 17.6 %copy-start.26 = (s32[96]{0:T(128)S(1)}, s32[96]{0:T(128)}, u32[]{:S(2)}) copy-start(s32[96]{0:T(128)} %param.13) | copy-start | bytes 1156
  7.8 19.3 %copy-start.1 = (f32[1,7,256,256]{3,2,1,0:T(8,128)S(1)}, f32[1,7,256,256]{3,2,1,0:T(8,128)}, u32[]{:S(2)}) copy-start(f32[1,7,256,256]{3,2,1,0:T(8,128)} %param.8) | copy-start | bytes 5505028
  7.8 19.3 %copy-start.6 = (f32[1,96,256]{2,1,0:T(8,128)S(1)}, f32[1,96,256]{2,1,0:T(8,128)}, u32[]{:S(2)}) copy-start(f32[1,96,256]{2,1,0:T(8,128)} %param.12) | copy-start | bytes 294916
  7.8 19.2 %copy-start.10 = (f32[1,256,256]{2,1,0:T(8,128)S(1)}, f32[1,256,256]{2,1,0:T(8,128)}, u32[]{:S(2)}) copy-start(f32[1,256,256]{2,1,0:T(8,128)} %param.7) | copy-start | bytes 786436
  24.3 1.0 copy-start.25
  25.1 1.9 %collective-permute-start.1 = (f32[4,96,256]{2,1,0:T(8,128)}, f32[4,96,256]{2,1,0:T(8,128)S(1)}, u32[]{:S(2)}, u32[]{:S(2)}) collective-permute-start(f32[4,96,256]{2,1,0:T(8,128)} %slice_bitcast_fusion.1), channel_id=1, source_target_pairs={{0,1},{1,0},{2,3},{3,2},{4,5},{5,4},{6,7},{7,6},{8,9},{9,8},{10,11... | collective-permute-start | bytes 1179656 | tf_op jit(solution)/shard_map/ppermute | solution.py:292
  31.4 19.1 %copy-start.12 = (f32[96,256]{1,0:T(8,128)}, f32[96,256]{1,0:T(8,128)S(1)}, u32[]{:S(2)}) copy-start(f32[96,256]{1,0:T(8,128)S(1)} %get-tuple-element.18.panel.residual) | copy-start | bytes 294916
  31.4 1.8 %collective-permute-start.2 = (f32[4,96,256]{2,1,0:T(8,128)S(1)}, f32[4,96,256]{2,1,0:T(8,128)S(1)}, u32[]{:S(2)}, u32[]{:S(2)}) collective-permute-start(f32[4,96,256]{2,1,0:T(8,128)S(1)} %get-tuple-element.20), channel_id=1, source_target_pairs={{0,1},{1,0},{2,3},{3,2},{4,5},{5,4},{6,7},{7,6},{8,9},{9,8},{10,11... | collective-permute-start | bytes 1179656 | tf_op jit(solution)/shard_map/ppermute | solution.py:289
  33.2 14.7 %copy-start.2 = (f32[1,7,256,256]{3,2,1,0:T(8,128)S(1)}, f32[1,7,256,256]{3,2,1,0:T(8,128)}, u32[]{:S(2)}) copy-start(f32[1,7,256,256]{3,2,1,0:T(8,128)} %param.11) | copy-start | bytes 5505028
  33.2 14.7 %copy-start.7 = (f32[1,256,256]{2,1,0:T(8,128)S(1)}, f32[1,256,256]{2,1,0:T(8,128)}, u32[]{:S(2)}) copy-start(f32[1,256,256]{2,1,0:T(8,128)} %param.10) | copy-start | bytes 786436
  47.8 2.7 %collective-permute-start.3 = (f32[4,96,256]{2,1,0:T(8,128)S(1)}, f32[4,96,256]{2,1,0:T(8,128)S(1)}, u32[]{:S(2)}, u32[]{:S(2)}) collective-permute-start(f32[4,96,256]{2,1,0:T(8,128)S(1)} %slice_bitcast_fusion), channel_id=1, source_target_pairs={{0,1},{1,0},{2,3},{3,2},{4,5},{5,4},{6,7},{7,6},{8,9},{9,8},{10,11... | collective-permute-start | bytes 1179656 | tf_op jit(solution)/shard_map/ppermute | solution.py:292
  50.4 3.2 %copy-start.17 = (f32[96,256]{1,0:T(8,128)}, f32[96,256]{1,0:T(8,128)S(1)}, u32[]{:S(2)}) copy-start(f32[96,256]{1,0:T(8,128)S(1)} %shard_map.91.newton_start) | copy-start | bytes 294916
  50.5 3.1 %copy-start.15 = (f32[4,96,256]{2,1,0:T(8,128)}, f32[4,96,256]{2,1,0:T(8,128)S(1)}, u32[]{:S(2)}) copy-start(f32[4,96,256]{2,1,0:T(8,128)S(1)} %collective-permute-done.3.other) | copy-start | bytes 1179652
  53.6 5.5 %copy-start.21 = (f32[96,256]{1,0:T(8,128)}, f32[96,256]{1,0:T(8,128)S(1)}, u32[]{:S(2)}) copy-start(f32[96,256]{1,0:T(8,128)S(1)} %get-tuple-element.21.image) | copy-start | bytes 294916
  53.6 5.5 %copy-start.23 = (f32[96,256]{1,0:T(8,128)}, f32[96,256]{1,0:T(8,128)S(1)}, u32[]{:S(2)}) copy-start(f32[96,256]{1,0:T(8,128)S(1)} %get-tuple-element.22.half_residual) | copy-start | bytes 294916
  54.3 23.3 %all-to-all-start.2 = ((f32[32,3,96]{2,1,0:T(4,128)}), f32[32,3,96]{2,1,0:T(4,128)}, u32[]{:S(2)}, u32[]{:S(2)}) async-start(f32[32,3,96]{2,1,0:T(4,128)} %broadcast_in_dim.30), calls=%async_computation.2 | async-start | bytes 131072 | tf_op jit(solution)/shard_map/all_to_all | solution.py:330
  70.1 1.5 %copy-start.3 = (f32[1,7,256,256]{3,2,1,0:T(8,128)S(1)}, f32[1,7,256,256]{3,2,1,0:T(8,128)}, u32[]{:S(2)}) copy-start(f32[1,7,256,256]{3,2,1,0:T(8,128)} %param.11) | copy-start | bytes 5505028
  71.6 0.9 copy-start.8
  73.5 1.0 copy-start.16
  77.6 1.5 %copy-start.4 = (f32[1,7,256,256]{3,2,1,0:T(8,128)S(1)}, f32[1,7,256,256]{3,2,1,0:T(8,128)}, u32[]{:S(2)}) copy-start(f32[1,7,256,256]{3,2,1,0:T(8,128)} %param.11) | copy-start | bytes 5505028
  79.1 0.9 copy-start.9
  91.9 15.1 %all-to-all-start.3 = ((f32[32,16,128]{2,1,0:T(8,128)}), f32[32,16,128]{2,1,0:T(8,128)S(1)}, u32[]{:S(2)}, u32[]{:S(2)}) async-start(f32[32,16,128]{2,1,0:T(8,128)} %get-tuple-element.27), calls=%async_computation.3 | async-start | bytes 524288 | tf_op jit(solution)/shard_map/all_to_all | solution.py:363
  (9 other events, 7.8 us)
